TPU v7x, 256 devices: a whole 4x4x8 slice. The times are simulated.
256 devices in a mesh: epoch: 16 (over x, y), row: 16 (over z, core).
Axes of the slice: x: 4, y: 4, z: 8, core: 2. Of those that a mesh axis runs over, the one named last changes fastest.
Arguments:
- forcing: float32 [16, 2, 128, 6144], P('epoch', None, 'row'), may hold values from -2400 to 2400
- observed: float32 [16, 2, 128, 6144], P('epoch', None, 'row'), may hold values from -6 to 6
- log_friction: float32 [128, 6144], P('row'), may hold values from -1.5 to 1.5
- log_rheology: float32 [128, 6144], P('row'), may hold values from -0.7 to 0.7
- grounded: int32 [128, 6144], P('row'), may hold values 0 or 1
Outputs:
- new_friction: float32 [128, 6144], P('row')
- new_rheology: float32 [128, 6144], P('row')
All inputs are finite; a program needn't handle non-finite values. No bound on the sum of `grounded` on one device may be relied on, other than what follows from the above.
Results may differ from a plain program's by a relative error of at most 0.00011.
Values sent between devices are 32-bit elements; how exact they have to be, the bound alone decides.
A program may use at most 64 MiB of HBM per device.

v0:
```python
import jax
import jax.numpy as jnp
from jax import lax
from jax.sharding import PartitionSpec as P

SWEEPS = 4


relax = 0.9
coupling = 0.1
step_size = 0.5


def padded(x, sides, width):
    for axis, dim in sides:
        devices, length = (lax.axis_size(axis), x.shape[dim])
        up = [(i, (i + 1) % devices) for i in range(devices - 1)]
        down = [(j, i) for i, j in up]
        last = lax.slice_in_dim(x, length - width, length, axis=dim)
        first = lax.slice_in_dim(x, 0, width, axis=dim)
        before = lax.ppermute(last, axis, up)
        after = lax.ppermute(first, axis, down)
        x = jnp.concatenate([before, x, after], axis=dim)
    return x


def shift_east(field):
    widths = [(0, 0)] * (field.ndim - 1) + [(0, 1)]
    return jnp.pad(field[..., 1:], widths)


def shift_west(field):
    widths = [(0, 0)] * (field.ndim - 1) + [(1, 0)]
    return jnp.pad(field[..., :-1], widths)


def cross_term(padded_comp):
    return (
        shift_east(padded_comp[2:])
        - shift_west(padded_comp[2:])
        - shift_east(padded_comp[:-2])
        + shift_west(padded_comp[:-2])
    )


def jacobi_sweep(padded_velocity, padded_stiffness, friction_coef, forcing_now):
    centre = padded_stiffness[1:-1]
    face_east = 0.5 * (centre + shift_east(centre))
    face_west = 0.5 * (centre + shift_west(centre))
    face_north = 0.5 * (centre + padded_stiffness[:-2])
    face_south = 0.5 * (centre + padded_stiffness[2:])
    along_sum = face_east + face_west
    across = face_north + face_south
    diag_u = 4.0 * along_sum + across + friction_coef + 0.5
    diag_v = along_sum + 4.0 * across + friction_coef + 0.5
    padded_u = padded_velocity[0]
    padded_v = padded_velocity[1]
    inner_u = padded_u[1:-1]
    inner_v = padded_v[1:-1]
    lateral_u = face_east * shift_east(inner_u) + face_west * shift_west(inner_u)
    vertical_u = face_north * padded_u[:-2] + face_south * padded_u[2:]
    lateral_v = face_east * shift_east(inner_v) + face_west * shift_west(inner_v)
    vertical_v = face_north * padded_v[:-2] + face_south * padded_v[2:]
    image_u = (
        diag_u * inner_u - 4.0 * lateral_u - vertical_u - coupling * centre * cross_term(padded_v)
    )
    image_v = (
        diag_v * inner_v - lateral_v - 4.0 * vertical_v - coupling * centre * cross_term(padded_u)
    )
    new_u = inner_u + relax * (forcing_now[0] - image_u) / diag_u
    new_v = inner_v + relax * (forcing_now[1] - image_v) / diag_v
    return jnp.stack([new_u, new_v])


def on_device(forcing, observed, log_friction, log_rheology, grounded):
    forcing_now = forcing[0]
    target = observed[0]
    stiffness = jnp.exp(log_rheology)
    friction_coef = grounded.astype(jnp.float32) * jnp.exp(log_friction)
    row_count = stiffness.shape[0]
    padded_stiffness = padded(stiffness, (("row", 0),), 1)
    velocity = jnp.zeros(forcing_now.shape, jnp.float32)
    saved_states = []
    for sweep_index in range(SWEEPS):
        padded_velocity = padded(velocity, (("row", 1),), 1)
        saved_states.append(padded_velocity)
        velocity = jacobi_sweep(padded_velocity, padded_stiffness, friction_coef, forcing_now)
    adjoint = velocity - target
    stiff_back = jnp.zeros(padded_stiffness.shape, jnp.float32)
    friction_back = jnp.zeros(friction_coef.shape, jnp.float32)

    def local_sweep(padded_state, padded_stiff, friction_field):
        return jacobi_sweep(padded_state, padded_stiff, friction_field, forcing_now)

    for sweep_index in reversed(range(SWEEPS)):
        unused, pullback = jax.vjp(
            local_sweep, saved_states[sweep_index], padded_stiffness, friction_coef
        )
        state_back, stiff_part, friction_part = pullback(adjoint)
        stiff_back = stiff_back + stiff_part
        friction_back = friction_back + friction_part
        if sweep_index > 0:
            edge_rows = jnp.concatenate([state_back[:, :1], state_back[:, -1:]], axis=1)
            received = padded(edge_rows, (("row", 1),), 1)
            adjoint = (
                state_back[:, 1:-1]
                + jnp.pad(received[:, :1], ((0, 0), (0, row_count - 1), (0, 0)))
                + jnp.pad(received[:, 3:], ((0, 0), (row_count - 1, 0), (0, 0)))
            )
    stiff_edges = jnp.concatenate([stiff_back[:1], stiff_back[-1:]], axis=0)
    stiff_received = padded(stiff_edges, (("row", 0),), 1)
    grad_stiff = (
        stiff_back[1:-1]
        + jnp.pad(stiff_received[:1], ((0, row_count - 1), (0, 0)))
        + jnp.pad(stiff_received[3:], ((row_count - 1, 0), (0, 0)))
    )
    gradient = jnp.stack([friction_back * friction_coef, grad_stiff * stiffness])
    parameters = jnp.stack([log_friction, log_rheology])
    cell_count = row_count * lax.axis_size("row") * gradient.shape[2]
    summed = lax.psum(gradient, "epoch")
    squares = lax.psum(jnp.sum(summed * summed, axis=(1, 2)), "row")
    grad_scale = jnp.sqrt(squares / cell_count + 1e-06)
    updated = parameters - step_size * summed / grad_scale[:, None, None]
    return (updated[0], updated[1])


def solution(mesh):
    in_specs = (
        P("epoch", None, "row", None),
        P("epoch", None, "row", None),
        P("row", None),
        P("row", None),
        P("row", None),
    )
    out_specs = (P("row", None), P("row", None))
    return jax.shard_map(
        on_device, mesh=mesh, in_specs=in_specs, out_specs=out_specs, check_vma=False
    )
```

profile of v0, /device:TPU:1, one launch (start us, length us, event | category | flops | bytes accessed | tf_op | source)
XLA Modules:
  0.0 230.6 jit_solution(5686686242233176888)
XLA Ops:
  7.2 5.1 %collective-permute-start.3 = (f32[2,1,6144]{2,1,0:T(1,128)S(1)}, f32[2,1,6144]{2,1,0:T(1,128)S(1)}, u32[]{:S(2)}, u32[]{:S(2)}) collective-permute-start(f32[2,1,6144]{2,1,0:T(1,128)S(1)} %broadcast.392), channel_id=1, source_target_pairs={{1,0},{2,1},{3,2},{4,3},{5,4},{6,5},{7,6},{8,7},{9,8},{10,9},{11,1... | collective-permute-start | bytes 147464 | tf_op jit(solution)/shard_map/ppermute | solution.py:22
  12.4 1.9 collective-permute-start.2
  14.3 1.0 exp.6
  15.3 2.2 collective-permute-start
  17.5 2.1 collective-permute-start.1
  19.9 0.2 fusion.149
  20.2 0.2 fusion.148
  20.4 2.3 collective-permute-done.1
  22.7 0.4 fusion.115
  23.3 0.4 fusion.117
  23.7 1.9 collective-permute-start.5
  25.7 3.6 %collective-permute-start.4 = (f32[2,1,6144]{2,1,0:T(1,128)S(1)}, f32[2,1,6144]{2,1,0:T(1,128)S(1)}, u32[]{:S(2)}, u32[]{:S(2)}) collective-permute-start(f32[2,1,6144]{2,1,0:T(1,128)S(1)} %get-tuple-element.122), channel_id=1, source_target_pairs={{0,1},{1,2},{2,3},{3,4},{4,5},{5,6},{6,7},{7,8},{8,9},{9,10},{10,1... | collective-permute-start | bytes 147464 | tf_op jit(solution)/shard_map/ppermute | solution.py:21
  29.4 1.0 collective-permute-done.4
  30.8 0.4 divide_add_fusion.3
  31.5 0.3 divide_add_fusion.2
  31.9 1.9 collective-permute-start.7
  33.8 4.2 %collective-permute-start.6 = (f32[2,1,6144]{2,1,0:T(1,128)S(1)}, f32[2,1,6144]{2,1,0:T(1,128)S(1)}, u32[]{:S(2)}, u32[]{:S(2)}) collective-permute-start(f32[2,1,6144]{2,1,0:T(1,128)S(1)} %get-tuple-element.118), channel_id=1, source_target_pairs={{0,1},{1,2},{2,3},{3,4},{4,5},{5,6},{6,7},{7,8},{8,9},{9,10},{10,1... | collective-permute-start | bytes 147464 | tf_op jit(solution)/shard_map/ppermute | solution.py:21
  38.2 1.0 collective-permute-done.6
  39.6 0.4 divide_add_fusion.1
  40.3 0.3 divide_add_fusion
  40.7 4.2 %collective-permute-start.8 = (f32[2,1,6144]{2,1,0:T(1,128)S(1)}, f32[2,1,6144]{2,1,0:T(1,128)S(1)}, u32[]{:S(2)}, u32[]{:S(2)}) collective-permute-start(f32[2,1,6144]{2,1,0:T(1,128)S(1)} %get-tuple-element.113), channel_id=1, source_target_pairs={{0,1},{1,2},{2,3},{3,4},{4,5},{5,6},{6,7},{7,8},{8,9},{9,10},{10,1... | collective-permute-start | bytes 147464 | tf_op jit(solution)/shard_map/ppermute | solution.py:21
  45.0 1.9 collective-permute-start.9
  47.0 3.4 %collective-permute-done.9 = f32[2,1,6144]{2,1,0:T(1,128)S(1)} collective-permute-done((f32[2,1,6144]{2,1,0:T(1,128)S(1)}, f32[2,1,6144]{2,1,0:T(1,128)S(1)}, u32[]{:S(2)}, u32[]{:S(2)}) %collective-permute-start.9) | collective-permute-done | bytes 49184 | tf_op jit(solution)/shard_map/ppermute | solution.py:22
  50.7 0.4 add_bitcast_fusion.1
  51.3 0.3 add_bitcast_fusion
  51.6 0.6 copy-done.5
  53.5 0.2 multiply_multiply_fusion.5
  53.7 0.2 fusion.28
  53.9 0.2 fusion.32
  54.2 1.9 collective-permute-start.10
  56.1 2.4 %collective-permute-start.11 = (f32[2,1,6144]{2,1,0:T(1,128)S(1)}, f32[2,1,6144]{2,1,0:T(1,128)S(1)}, u32[]{:S(2)}, u32[]{:S(2)}) collective-permute-start(f32[2,1,6144]{2,1,0:T(1,128)S(1)} %get-tuple-element.93), channel_id=1, source_target_pairs={{1,0},{2,1},{3,2},{4,3},{5,4},{6,5},{7,6},{8,7},{9,8},{10,9},{11,1... | collective-permute-start | bytes 147464 | tf_op jit(solution)/shard_map/ppermute | solution.py:22
  58.6 3.3 %collective-permute-done.11 = f32[2,1,6144]{2,1,0:T(1,128)S(1)} collective-permute-done((f32[2,1,6144]{2,1,0:T(1,128)S(1)}, f32[2,1,6144]{2,1,0:T(1,128)S(1)}, u32[]{:S(2)}, u32[]{:S(2)}) %collective-permute-start.11) | collective-permute-done | bytes 49184 | tf_op jit(solution)/shard_map/ppermute | solution.py:22
  62.1 0.2 slice_multiply_fusion.5
  62.4 0.2 slice_multiply_fusion.7
  63.1 0.2 multiply_multiply_fusion.3
  63.3 0.2 fusion.20
  63.5 0.2 fusion.24
  63.8 1.9 collective-permute-start.12
  65.8 2.4 %collective-permute-start.13 = (f32[2,1,6144]{2,1,0:T(1,128)S(1)}, f32[2,1,6144]{2,1,0:T(1,128)S(1)}, u32[]{:S(2)}, u32[]{:S(2)}) collective-permute-start(f32[2,1,6144]{2,1,0:T(1,128)S(1)} %get-tuple-element.91), channel_id=1, source_target_pairs={{1,0},{2,1},{3,2},{4,3},{5,4},{6,5},{7,6},{8,7},{9,8},{10,9},{11,1... | collective-permute-start | bytes 147464 | tf_op jit(solution)/shard_map/ppermute | solution.py:22
  68.2 6.1 %collective-permute-done.13 = f32[2,1,6144]{2,1,0:T(1,128)S(1)} collective-permute-done((f32[2,1,6144]{2,1,0:T(1,128)S(1)}, f32[2,1,6144]{2,1,0:T(1,128)S(1)}, u32[]{:S(2)}, u32[]{:S(2)}) %collective-permute-start.13) | collective-permute-done | bytes 49184 | tf_op jit(solution)/shard_map/ppermute | solution.py:22
  74.5 0.2 slice_multiply_fusion.1
  75.5 0.2 multiply_multiply_fusion.1
  75.7 0.2 fusion.12
  76.0 0.2 fusion.16
  76.3 2.3 %collective-permute-start.14 = (f32[2,1,6144]{2,1,0:T(1,128)S(1)}, f32[2,1,6144]{2,1,0:T(1,128)S(1)}, u32[]{:S(2)}, u32[]{:S(2)}) collective-permute-start(f32[2,1,6144]{2,1,0:T(1,128)S(1)} %get-tuple-element.88), channel_id=1, source_target_pairs={{0,1},{1,2},{2,3},{3,4},{4,5},{5,6},{6,7},{7,8},{8,9},{9,10},{10,1... | collective-permute-start | bytes 147464 | tf_op jit(solution)/shard_map/ppermute | solution.py:21
  78.6 2.2 collective-permute-start.15
  80.8 7.6 %collective-permute-done.15 = f32[2,1,6144]{2,1,0:T(1,128)S(1)} collective-permute-done((f32[2,1,6144]{2,1,0:T(1,128)S(1)}, f32[2,1,6144]{2,1,0:T(1,128)S(1)}, u32[]{:S(2)}, u32[]{:S(2)}) %collective-permute-start.15) | collective-permute-done | bytes 49184 | tf_op jit(solution)/shard_map/ppermute | solution.py:22
  88.5 0.5 multiply_bitcast_fusion
  89.0 0.2 add_multiply_fusion.13
  89.3 0.2 add_multiply_fusion.9
  89.7 0.2 add_multiply_fusion.5
  90.2 0.2 fusion.77
  90.4 0.2 fusion.72
  90.6 0.2 fusion.67
  90.8 0.2 fusion.62
  91.2 1.9 collective-permute-start.16
  93.1 2.4 %collective-permute-start.17 = (f32[1,6144]{1,0:T(1,128)S(1)}, f32[1,6144]{1,0:T(1,128)S(1)}, u32[]{:S(2)}, u32[]{:S(2)}) collective-permute-start(f32[1,6144]{1,0:T(1,128)S(1)} %add_add_fusion.3), channel_id=1, source_target_pairs={{1,0},{2,1},{3,2},{4,3},{5,4},{6,5},{7,6},{8,7},{9,8},{10,9},{11,1... | collective-permute-start | bytes 73736 | tf_op jit(solution)/shard_map/ppermute | solution.py:22
  95.5 0.3 add_add_fusion
  95.9 3.6 %collective-permute-done.17 = f32[1,6144]{1,0:T(1,128)S(1)} collective-permute-done((f32[1,6144]{1,0:T(1,128)S(1)}, f32[1,6144]{1,0:T(1,128)S(1)}, u32[]{:S(2)}, u32[]{:S(2)}) %collective-permute-start.17) | collective-permute-done | bytes 24608 | tf_op jit(solution)/shard_map/ppermute | solution.py:22
  99.5 0.8 pad_maximum_fusion
  100.4 95.9 %all-reduce.164.cloned.1.call-done = f32[2,8,6144]{2,1,0:T(8,128)} async-done(((f32[2,8,6144]{2,1,0:T(8,128)}), f32[2,8,6144]{2,1,0:T(8,128)}) %all-reduce.164.cloned.1.call-update) | async-done | bytes 393232 | tf_op jit(solution)/shard_map/psum | solution.py:120
  196.3 1.2 multiply_reduce_fusion
  197.5 25.3 %psum.15 = f32[2]{0:T(128)S(1)} all-reduce(f32[2]{0:T(128)S(1)} %multiply_reduce_fusion), channel_id=1, replica_groups=mesh['epoch'=16,'row'=16] {'row'}, use_global_device_ids=true, to_apply=%region_2.3 | all-reduce | flops 2 | bytes 16 | tf_op jit(solution)/shard_map/psum | solution.py:121
  223.0 0.8 slice_bitcast_fusion
  (98 shorter events, 7.0 us)
Async XLA Ops:
  7.2 189.2 %all-reduce.164.cloned.1.call-start = ((), (), s32[]{:S(2)}) async-start(), calls=%async_computation | async-start | bytes 786432 | tf_op jit(solution)/shard_map/psum | solution.py:120
  7.2 12.9 %collective-permute-start.3 = (f32[2,1,6144]{2,1,0:T(1,128)S(1)}, f32[2,1,6144]{2,1,0:T(1,128)S(1)}, u32[]{:S(2)}, u32[]{:S(2)}) collective-permute-start(f32[2,1,6144]{2,1,0:T(1,128)S(1)} %broadcast.392), channel_id=1, source_target_pairs={{1,0},{2,1},{3,2},{4,3},{5,4},{6,5},{7,6},{8,7},{9,8},{10,9},{11,1... | collective-permute-start | bytes 147464 | tf_op jit(solution)/shard_map/ppermute | solution.py:22
  12.4 7.5 %collective-permute-start.2 = (f32[2,1,6144]{2,1,0:T(1,128)S(1)}, f32[2,1,6144]{2,1,0:T(1,128)S(1)}, u32[]{:S(2)}, u32[]{:S(2)}) collective-permute-start(f32[2,1,6144]{2,1,0:T(1,128)S(1)} %broadcast.392), channel_id=1, source_target_pairs={{0,1},{1,2},{2,3},{3,4},{4,5},{5,6},{6,7},{7,8},{8,9},{9,10},{10,1... | collective-permute-start | bytes 147464 | tf_op jit(solution)/shard_map/ppermute | solution.py:21
  15.3 5.1 %collective-permute-start = (f32[1,6144]{1,0:T(1,128)S(1)}, f32[1,6144]{1,0:T(1,128)S(1)}, u32[]{:S(2)}, u32[]{:S(2)}) collective-permute-start(f32[1,6144]{1,0:T(1,128)S(1)} %get-tuple-element.211), channel_id=1, source_target_pairs={{0,1},{1,2},{2,3},{3,4},{4,5},{5,6},{6,7},{7,8},{8,9},{9,10},{10,1... | collective-permute-start | bytes 73736 | tf_op jit(solution)/shard_map/ppermute | solution.py:21
  17.5 5.1 %collective-permute-start.1 = (f32[1,6144]{1,0:T(1,128)S(1)}, f32[1,6144]{1,0:T(1,128)S(1)}, u32[]{:S(2)}, u32[]{:S(2)}) collective-permute-start(f32[1,6144]{1,0:T(1,128)S(1)} %get-tuple-element.212), channel_id=1, source_target_pairs={{1,0},{2,1},{3,2},{4,3},{5,4},{6,5},{7,6},{8,7},{9,8},{10,9},{11,1... | collective-permute-start | bytes 73736 | tf_op jit(solution)/shard_map/ppermute | solution.py:22
  20.2 2.5 %copy-start = (f32[8,6144]{1,0:T(8,128)S(1)}, f32[8,6144]{1,0:T(8,128)}, u32[]{:S(2)}) copy-start(f32[8,6144]{1,0:T(8,128)} %param.8) | copy-start | bytes 589828
  20.2 2.5 %copy-start.1 = (f32[1,2,8,6144]{3,2,1,0:T(8,128)S(1)}, f32[1,2,8,6144]{3,2,1,0:T(8,128)}, u32[]{:S(2)}) copy-start(f32[1,2,8,6144]{3,2,1,0:T(8,128)} %param.5) | copy-start | bytes 1179652
  20.2 2.5 %copy-start.2 = (f32[8,6144]{1,0:T(8,128)S(1)}, f32[8,6144]{1,0:T(8,128)}, u32[]{:S(2)}) copy-start(f32[8,6144]{1,0:T(8,128)} %param.7) | copy-start | bytes 589828
  20.2 2.5 %copy-start.3 = (s32[8,6144]{1,0:T(8,128)S(1)}, s32[8,6144]{1,0:T(8,128)}, u32[]{:S(2)}) copy-start(s32[8,6144]{1,0:T(8,128)} %param.9) | copy-start | bytes 589828
  23.7 5.7 %collective-permute-start.5 = (f32[2,1,6144]{2,1,0:T(1,128)S(1)}, f32[2,1,6144]{2,1,0:T(1,128)S(1)}, u32[]{:S(2)}, u32[]{:S(2)}) collective-permute-start(f32[2,1,6144]{2,1,0:T(1,128)S(1)} %get-tuple-element.121), channel_id=1, source_target_pairs={{1,0},{2,1},{3,2},{4,3},{5,4},{6,5},{7,6},{8,7},{9,8},{10,9},{11,1... | collective-permute-start | bytes 147464 | tf_op jit(solution)/shard_map/ppermute | solution.py:22
  25.7 4.8 %collective-permute-start.4 = (f32[2,1,6144]{2,1,0:T(1,128)S(1)}, f32[2,1,6144]{2,1,0:T(1,128)S(1)}, u32[]{:S(2)}, u32[]{:S(2)}) collective-permute-start(f32[2,1,6144]{2,1,0:T(1,128)S(1)} %get-tuple-element.122), channel_id=1, source_target_pairs={{0,1},{1,2},{2,3},{3,4},{4,5},{5,6},{6,7},{7,8},{8,9},{9,10},{10,1... | collective-permute-start | bytes 147464 | tf_op jit(solution)/shard_map/ppermute | solution.py:21
  31.9 6.3 %collective-permute-start.7 = (f32[2,1,6144]{2,1,0:T(1,128)S(1)}, f32[2,1,6144]{2,1,0:T(1,128)S(1)}, u32[]{:S(2)}, u32[]{:S(2)}) collective-permute-start(f32[2,1,6144]{2,1,0:T(1,128)S(1)} %get-tuple-element.117), channel_id=1, source_target_pairs={{1,0},{2,1},{3,2},{4,3},{5,4},{6,5},{7,6},{8,7},{9,8},{10,9},{11,1... | collective-permute-start | bytes 147464 | tf_op jit(solution)/shard_map/ppermute | solution.py:22
  33.8 5.4 %collective-permute-start.6 = (f32[2,1,6144]{2,1,0:T(1,128)S(1)}, f32[2,1,6144]{2,1,0:T(1,128)S(1)}, u32[]{:S(2)}, u32[]{:S(2)}) collective-permute-start(f32[2,1,6144]{2,1,0:T(1,128)S(1)} %get-tuple-element.118), channel_id=1, source_target_pairs={{0,1},{1,2},{2,3},{3,4},{4,5},{5,6},{6,7},{7,8},{8,9},{9,10},{10,1... | collective-permute-start | bytes 147464 | tf_op jit(solution)/shard_map/ppermute | solution.py:21
  40.7 6.3 %collective-permute-start.8 = (f32[2,1,6144]{2,1,0:T(1,128)S(1)}, f32[2,1,6144]{2,1,0:T(1,128)S(1)}, u32[]{:S(2)}, u32[]{:S(2)}) collective-permute-start(f32[2,1,6144]{2,1,0:T(1,128)S(1)} %get-tuple-element.113), channel_id=1, source_target_pairs={{0,1},{1,2},{2,3},{3,4},{4,5},{5,6},{6,7},{7,8},{8,9},{9,10},{10,1... | collective-permute-start | bytes 147464 | tf_op jit(solution)/shard_map/ppermute | solution.py:21
  45.0 5.4 %collective-permute-start.9 = (f32[2,1,6144]{2,1,0:T(1,128)S(1)}, f32[2,1,6144]{2,1,0:T(1,128)S(1)}, u32[]{:S(2)}, u32[]{:S(2)}) collective-permute-start(f32[2,1,6144]{2,1,0:T(1,128)S(1)} %get-tuple-element.114), channel_id=1, source_target_pairs={{1,0},{2,1},{3,2},{4,3},{5,4},{6,5},{7,6},{8,7},{9,8},{10,9},{11,1... | collective-permute-start | bytes 147464 | tf_op jit(solution)/shard_map/ppermute | solution.py:22
  51.3 1.0 copy-start.5
  54.2 4.3 %collective-permute-start.10 = (f32[2,1,6144]{2,1,0:T(1,128)S(1)}, f32[2,1,6144]{2,1,0:T(1,128)S(1)}, u32[]{:S(2)}, u32[]{:S(2)}) collective-permute-start(f32[2,1,6144]{2,1,0:T(1,128)S(1)} %get-tuple-element.92), channel_id=1, source_target_pairs={{0,1},{1,2},{2,3},{3,4},{4,5},{5,6},{6,7},{7,8},{8,9},{9,10},{10,1... | collective-permute-start | bytes 147464 | tf_op jit(solution)/shard_map/ppermute | solution.py:21
  56.1 5.7 %collective-permute-start.11 = (f32[2,1,6144]{2,1,0:T(1,128)S(1)}, f32[2,1,6144]{2,1,0:T(1,128)S(1)}, u32[]{:S(2)}, u32[]{:S(2)}) collective-permute-start(f32[2,1,6144]{2,1,0:T(1,128)S(1)} %get-tuple-element.93), channel_id=1, source_target_pairs={{1,0},{2,1},{3,2},{4,3},{5,4},{6,5},{7,6},{8,7},{9,8},{10,9},{11,1... | collective-permute-start | bytes 147464 | tf_op jit(solution)/shard_map/ppermute | solution.py:22
  63.8 4.3 %collective-permute-start.12 = (f32[2,1,6144]{2,1,0:T(1,128)S(1)}, f32[2,1,6144]{2,1,0:T(1,128)S(1)}, u32[]{:S(2)}, u32[]{:S(2)}) collective-permute-start(f32[2,1,6144]{2,1,0:T(1,128)S(1)} %get-tuple-element.90), channel_id=1, source_target_pairs={{0,1},{1,2},{2,3},{3,4},{4,5},{5,6},{6,7},{7,8},{8,9},{9,10},{10,1... | collective-permute-start | bytes 147464 | tf_op jit(solution)/shard_map/ppermute | solution.py:21
  65.8 8.5 %collective-permute-start.13 = (f32[2,1,6144]{2,1,0:T(1,128)S(1)}, f32[2,1,6144]{2,1,0:T(1,128)S(1)}, u32[]{:S(2)}, u32[]{:S(2)}) collective-permute-start(f32[2,1,6144]{2,1,0:T(1,128)S(1)} %get-tuple-element.91), channel_id=1, source_target_pairs={{1,0},{2,1},{3,2},{4,3},{5,4},{6,5},{7,6},{8,7},{9,8},{10,9},{11,1... | collective-permute-start | bytes 147464 | tf_op jit(solution)/shard_map/ppermute | solution.py:22
  76.3 4.5 %collective-permute-start.14 = (f32[2,1,6144]{2,1,0:T(1,128)S(1)}, f32[2,1,6144]{2,1,0:T(1,128)S(1)}, u32[]{:S(2)}, u32[]{:S(2)}) collective-permute-start(f32[2,1,6144]{2,1,0:T(1,128)S(1)} %get-tuple-element.88), channel_id=1, source_target_pairs={{0,1},{1,2},{2,3},{3,4},{4,5},{5,6},{6,7},{7,8},{8,9},{9,10},{10,1... | collective-permute-start | bytes 147464 | tf_op jit(solution)/shard_map/ppermute | solution.py:21
  78.6 9.8 %collective-permute-start.15 = (f32[2,1,6144]{2,1,0:T(1,128)S(1)}, f32[2,1,6144]{2,1,0:T(1,128)S(1)}, u32[]{:S(2)}, u32[]{:S(2)}) collective-permute-start(f32[2,1,6144]{2,1,0:T(1,128)S(1)} %get-tuple-element.89), channel_id=1, source_target_pairs={{1,0},{2,1},{3,2},{4,3},{5,4},{6,5},{7,6},{8,7},{9,8},{10,9},{11,1... | collective-permute-start | bytes 147464 | tf_op jit(solution)/shard_map/ppermute | solution.py:22
  91.2 4.7 %collective-permute-start.16 = (f32[1,6144]{1,0:T(1,128)S(1)}, f32[1,6144]{1,0:T(1,128)S(1)}, u32[]{:S(2)}, u32[]{:S(2)}) collective-permute-start(f32[1,6144]{1,0:T(1,128)S(1)} %add_add_fusion.4), channel_id=1, source_target_pairs={{0,1},{1,2},{2,3},{3,4},{4,5},{5,6},{6,7},{7,8},{8,9},{9,10},{10,1... | collective-permute-start | bytes 73736 | tf_op jit(solution)/shard_map/ppermute | solution.py:21
  93.1 6.4 %collective-permute-start.17 = (f32[1,6144]{1,0:T(1,128)S(1)}, f32[1,6144]{1,0:T(1,128)S(1)}, u32[]{:S(2)}, u32[]{:S(2)}) collective-permute-start(f32[1,6144]{1,0:T(1,128)S(1)} %add_add_fusion.3), channel_id=1, source_target_pairs={{1,0},{2,1},{3,2},{4,3},{5,4},{6,5},{7,6},{8,7},{9,8},{10,9},{11,1... | collective-permute-start | bytes 73736 | tf_op jit(solution)/shard_map/ppermute | solution.py:22
  196.3 26.5 %copy-start.4 = (f32[2,8,6144]{2,1,0:T(8,128)S(1)}, f32[2,8,6144]{2,1,0:T(8,128)}, u32[]{:S(2)}) copy-start(f32[2,8,6144]{2,1,0:T(8,128)} %all-reduce.164.cloned.1.call-done) | copy-start | bytes 1179652
Sparse Core Ops, SparseCore 0:
  100.5 95.7 all-reduce.163
where the time goes:
time: 231 us
  waiting for transfers between devices  124 us (54%)
  starting transfers between devices  46.8 us (20%)
  blocking collectives  25.3 us (11%)
  between operations  14.9 us (6%)
  other arithmetic  12.6 us (5%)
  local copies, waits for them, and re-layouts  6.81 us (3%)
    psum x1, waiting for transfers between devices, on_device(): summed = lax.psum(gradient, 'epoch')  95.9 us
    ppermute x9, waiting for transfers between devices, padded(): after = lax.ppermute(first, axis, down)  26.1 us
    psum x1, blocking collectives, on_device(): squares = lax.psum(jnp.sum(summed * summed, axis=(1, 2)), 'row')  25.3 us
    ppermute x9, starting transfers between devices, padded(): before = lax.ppermute(last, axis, up)  24.3 us
    ppermute x9, starting transfers between devices, padded(): after = lax.ppermute(first, axis, down)  22.4 us
  transfers between devices with their start and end apart: 19, of which 9 were waited for; matrix products, arithmetic and copies ran while one was open for 1% of the time, Pallas kernels for 0%

commit v1 on v0

v1 whole, which is shorter than its diff:
```python
import math

import jax
import jax.numpy as jnp
from jax import lax
from jax.experimental import pallas as pl
from jax.experimental.pallas import tpu as pltpu
from jax.sharding import PartitionSpec as P

relax = 0.9
coupling = 0.1
step_size = 0.5
keep = 1.0 - relax

MESH = pl.DeviceIdType.MESH
ROWS = 8
OFF = 4
HELD = ROWS + 2 * OFF
SUB, LANE = 8, 128


def make_kernel(n_epoch, n_row, cols):
    pieces = cols // (SUB * LANE)
    span = pieces * SUB
    side = math.isqrt(n_epoch)
    cells = n_row * ROWS * cols

    def kernel(
        f_in, o_in, lf_in, lr_in, gr_in, outq, outr,
        fraw, oraw, lfraw, lrraw, grraw,
        stiff, fric, force, fe, fw, fn, fs, m01, rdu, rdv,
        v1, v2, v3, v4,
        l4, p4, q4, l3, p3, q3, l2, p2, q2,
        accn, accs, acce, accw, accc, accu, accv,
        facen, faces, own, grad, g4out, g4in,
        rsbuf, summed, total, sqout, sqin, rowout, rowin,
        load_sem, hsend, hrecv, asend, arecv, rsend, rrecv, gsend, grecv, ssend, srecv, tsend, trecv,
    ):
        me = lax.axis_index("row")
        ep = lax.axis_index("epoch")
        up = lax.rem(me + n_row - 1, n_row)
        down = lax.rem(me + 1, n_row)
        has_up = (me > 0).astype(jnp.float32)
        has_down = (me < n_row - 1).astype(jnp.float32)

        loads = [
            pltpu.make_async_copy(src, dst, load_sem.at[k])
            for k, (src, dst) in enumerate(
                ((lr_in, lrraw), (lf_in, lfraw), (gr_in, grraw), (f_in, fraw), (o_in, oraw))
            )
        ]
        for load in loads:
            load.start()

        ex, ey = ep // side, lax.rem(ep, side)
        peers = []
        for dx in range(side):
            for dy in range(side):
                if dx or dy:
                    peers.append(lax.rem(ex + dx, side) * side + lax.rem(ey + dy, side))

        barrier = pltpu.get_barrier_semaphore()
        for k in range(1, n_row):
            pl.semaphore_signal(
                barrier, inc=1, device_id={"row": lax.rem(me + k, n_row)}, device_id_type=MESH
            )
        for peer in peers:
            pl.semaphore_signal(barrier, inc=1, device_id={"epoch": peer}, device_id_type=MESH)

        lane = lax.broadcasted_iota(jnp.int32, (SUB, LANE), 1)
        sub = lax.broadcasted_iota(jnp.int32, (SUB, LANE), 0)
        last_lane, first_lane = lane == LANE - 1, lane == 0
        last_sub, first_sub = sub == SUB - 1, sub == 0
        zero = jnp.zeros((SUB, LANE), jnp.float32)
        every = range(pieces)

        def east(x):
            r = [pltpu.roll(p, LANE - 1, 1) for p in x]
            end = jnp.where(last_sub, zero, pltpu.roll(r[0], SUB - 1, 0))
            return [jnp.where(last_lane, r[k + 1] if k + 1 < pieces else end, r[k]) for k in every]

        def west(x):
            r = [pltpu.roll(p, 1, 1) for p in x]
            end = jnp.where(first_sub, zero, pltpu.roll(r[-1], 1, 0))
            return [jnp.where(first_lane, r[k - 1] if k else end, r[k]) for k in every]

        def lanes(k):
            return slice(k * LANE, (k + 1) * LANE)

        def get(ref, *at):
            return [ref[(*at, slice(None), lanes(k))] for k in every]

        def put(ref, x, *at):
            for k in every:
                ref[(*at, slice(None), lanes(k))] = x[k]

        def raw(ref, i, part=0):
            return [ref[pl.ds(part * span * SUB + k * SUB + i, SUB, stride=span), :] for k in every]

        def cross(north, south):
            d = [s - n for s, n in zip(south, north)]
            return [a - b for a, b in zip(east(d), west(d))]

        def rows(lo, hi, body):
            def step(a, carry):
                body(a)
                return carry

            lax.fori_loop(lo + OFF, hi + OFF, step, 0)

        loads[0].wait()

        def own_stiff(a):
            put(stiff, [jnp.exp(x) for x in raw(lrraw, a - OFF)], a)

        rows(0, ROWS, own_stiff)
        loads[1].wait()
        loads[2].wait()

        def own_fric(a):
            held_up = zip(raw(grraw, a - OFF), raw(lfraw, a - OFF))
            put(fric, [g.astype(jnp.float32) * jnp.exp(x) for g, x in held_up], a)

        rows(0, ROWS, own_fric)
        loads[3].wait()

        def own_force(a):
            put(force, raw(fraw, a - OFF, 0), a, 0)
            put(force, raw(fraw, a - OFF, 1), a, 1)

        rows(0, ROWS, own_force)

        pl.semaphore_wait(barrier, n_row - 1 + len(peers))

        def send(src, dst, ssem, rsem, where):
            copy = pltpu.make_async_remote_copy(
                src_ref=src, dst_ref=dst, send_sem=ssem, recv_sem=rsem,
                device_id=where, device_id_type=MESH,
            )
            copy.start()
            return copy

        halo = []
        for k, (ref, depth) in enumerate(((stiff, 4), (fric, 3), (force, 3))):
            halo.append(send(
                ref.at[pl.ds(OFF, depth)], ref.at[pl.ds(OFF + ROWS, depth)],
                hsend.at[2 * k], hrecv.at[2 * k], {"row": up},
            ))
            halo.append(send(
                ref.at[pl.ds(OFF + ROWS - depth, depth)], ref.at[pl.ds(OFF - depth, depth)],
                hsend.at[2 * k + 1], hrecv.at[2 * k + 1], {"row": down},
            ))

        def coefficients(a):
            c, n, s = get(stiff, a), get(stiff, a - 1), get(stiff, a + 1)
            he = [0.5 * (x + y) for x, y in zip(c, east(c))]
            hw = [0.5 * (x + y) for x, y in zip(c, west(c))]
            hn = [0.5 * (x + y) for x, y in zip(c, n)]
            hs = [0.5 * (x + y) for x, y in zip(c, s)]
            fr = get(fric, a)
            inside = relax * jnp.where(a < OFF, has_up, jnp.where(a >= OFF + ROWS, has_down, 1.0))
            put(fe, he, a)
            put(fw, hw, a)
            put(fn, hn, a)
            put(fs, hs, a)
            put(m01, [coupling * x for x in c], a)
            fu, fv = get(force, a, 0), get(force, a, 1)
            for k in every:
                along, across = he[k] + hw[k], hn[k] + hs[k]
                base = fr[k] + 0.5
                ru = inside / (4.0 * along + across + base)
                rv = inside / (along + 4.0 * across + base)
                rdu[a, :, lanes(k)] = ru
                rdv[a, :, lanes(k)] = rv
                v1[a, 0, :, lanes(k)] = ru * fu[k]
                v1[a, 1, :, lanes(k)] = rv * fv[k]

        def sweep(src, dst):
            def body(a):
                he, hw, hn, hs, m = get(fe, a), get(fw, a), get(fn, a), get(fs, a), get(m01, a)
                un, uc, us = get(src, a - 1, 0), get(src, a, 0), get(src, a + 1, 0)
                vn, vc, vs = get(src, a - 1, 1), get(src, a, 1), get(src, a + 1, 1)
                ue, uw, ve, vw = east(uc), west(uc), east(vc), west(vc)
                xu, xv = cross(un, us), cross(vn, vs)
                for k in every:
                    lat_u = he[k] * ue[k] + hw[k] * uw[k]
                    ver_u = hn[k] * un[k] + hs[k] * us[k]
                    lat_v = he[k] * ve[k] + hw[k] * vw[k]
                    ver_v = hn[k] * vn[k] + hs[k] * vs[k]
                    off_u = 4.0 * lat_u + ver_u + m[k] * xv[k]
                    off_v = lat_v + 4.0 * ver_v + m[k] * xu[k]
                    at = (slice(None), lanes(k))
                    dst[(a, 0, *at)] = keep * uc[k] + v1[(a, 0, *at)] + rdu[(a, *at)] * off_u
                    dst[(a, 1, *at)] = keep * vc[k] + v1[(a, 1, *at)] + rdv[(a, *at)] * off_v

            return body

        rows(1, ROWS - 1, coefficients)
        rows(2, ROWS - 2, sweep(v1, v2))
        rows(3, ROWS - 3, sweep(v2, v3))

        for copy in halo:
            copy.wait_recv()
        for k in every:
            stiff[OFF - 1, :, lanes(k)] = stiff[OFF - 1, :, lanes(k)] * has_up
            stiff[OFF + ROWS, :, lanes(k)] = stiff[OFF + ROWS, :, lanes(k)] * has_down
        rows(-3, 1, coefficients)
        rows(ROWS - 1, ROWS + 3, coefficients)
        for a in (0, HELD - 1):
            put(m01, [coupling * x for x in get(stiff, a)], a)
        rows(-2, 2, sweep(v1, v2))
        rows(ROWS - 2, ROWS + 2, sweep(v1, v2))
        rows(-1, 3, sweep(v2, v3))
        rows(ROWS - 3, ROWS + 1, sweep(v2, v3))
        rows(0, ROWS, sweep(v3, v4))

        loads[4].wait()

        def last_adjoint(a):
            m = get(m01, a)
            for comp, rd in ((0, rdu), (1, rdv)):
                lam = [x - y for x, y in zip(get(v4, a, comp), raw(oraw, a - OFF, comp))]
                p = [r * x for r, x in zip(get(rd, a), lam)]
                put(l4, lam, a, comp)
                put(p4, p, a, comp)
                put(q4, [x * y for x, y in zip(m, p)], a, comp)

        rows(0, ROWS, last_adjoint)
        back = [
            send(l4.at[pl.ds(OFF, 3)], l4.at[pl.ds(OFF + ROWS, 3)], asend.at[0], arecv.at[0], {"row": up}),
            send(l4.at[pl.ds(OFF + ROWS - 3, 3)], l4.at[pl.ds(OFF - 3, 3)], asend.at[1], arecv.at[1], {"row": down}),
            send(p4.at[pl.ds(OFF + 3, 1)], p4.at[pl.ds(OFF + ROWS + 3, 1)], asend.at[2], arecv.at[2], {"row": up}),
            send(p4.at[pl.ds(OFF + ROWS - 4, 1)], p4.at[pl.ds(0, 1)], asend.at[3], arecv.at[3], {"row": down}),
        ]

        def terms(a, p, before, after):
            pu, pv = get(p, a, 0), get(p, a, 1)
            un, uc, us = get(before, a - 1, 0), get(before, a, 0), get(before, a + 1, 0)
            vn, vc, vs = get(before, a - 1, 1), get(before, a, 1), get(before, a + 1, 1)
            ue, uw, ve, vw = east(uc), west(uc), east(vc), west(vc)
            xu, xv = cross(un, us), cross(vn, vs)
            au, av = get(after, a, 0), get(after, a, 1)
            out = []
            for k in every:
                pu4, pv4 = 4.0 * pu[k], 4.0 * pv[k]
                out.append((
                    pu[k] * un[k] + pv4 * vn[k],
                    pu[k] * us[k] + pv4 * vs[k],
                    pu4 * ue[k] + pv[k] * ve[k],
                    pu4 * uw[k] + pv[k] * vw[k],
                    pu[k] * xv[k] + pv[k] * xu[k],
                    pu[k] * (au[k] - keep * uc[k]),
                    pv[k] * (av[k] - keep * vc[k]),
                ))
            return out

        held = (accn, accs, acce, accw, accc, accu, accv)

        def last_terms(a):
            for k, values in enumerate(terms(a, p4, v3, v4)):
                for ref, value in zip(held, values):
                    ref[a, :, lanes(k)] = value

        rows(0, ROWS, last_terms)
        inv = 1.0 / relax
        for k in every:
            for slot, (a, ref) in enumerate(((OFF, accn), (OFF + ROWS - 1, accs))):
                at = (a, slice(None), lanes(k))
                g4out[slot, :, lanes(k)] = ref[at] - inv * (accu[at] + 4.0 * accv[at])
            for a in (OFF - 1, OFF + ROWS):
                for ref in held:
                    ref[a, :, lanes(k)] = zero
        back.append(send(g4out.at[0], g4in.at[1], asend.at[4], arecv.at[4], {"row": up}))
        back.append(send(g4out.at[1], g4in.at[0], asend.at[5], arecv.at[5], {"row": down}))

        def adjoint_row(a, lam, p, q):
            he, hw, hn, hs = get(fe, a), get(fw, a), get(fn, a), get(fs, a)
            result = []
            for comp, (along, across) in enumerate(((4.0, 1.0), (1.0, 4.0))):
                pn, pc, ps = get(p, a - 1, comp), get(p, a, comp), get(p, a + 1, comp)
                pe, pw = east(pc), west(pc)
                x = cross(get(q, a - 1, 1 - comp), get(q, a + 1, 1 - comp))
                la = get(lam, a, comp)
                new = []
                for k in every:
                    lat = he[k] * pe[k] + hw[k] * pw[k]
                    ver = hn[k] * pn[k] + hs[k] * ps[k]
                    lat = 4.0 * lat if comp == 0 else lat
                    ver = 4.0 * ver if comp == 1 else ver
                    new.append(keep * la[k] + lat + ver + x[k])
                result.append(new)
            return result

        def adjoint(lam, p, q, lam_to, p_to, q_to):
            def body(a):
                m = get(m01, a)
                for comp, (new, rd) in enumerate(zip(adjoint_row(a, lam, p, q), (rdu, rdv))):
                    pp = [r * x for r, x in zip(get(rd, a), new)]
                    put(lam_to, new, a, comp)
                    put(p_to, pp, a, comp)
                    put(q_to, [x * y for x, y in zip(m, pp)], a, comp)

            return body

        third = adjoint(l4, p4, q4, l3, p3, q3)
        second = adjoint(l3, p3, q3, l2, p2, q2)

        def finish(a):
            t3, t2 = terms(a, p3, v2, v3), terms(a, p2, v1, v2)
            l1 = adjoint_row(a, l2, p2, q2)
            east_part, west_part, rest = [], [], []
            for k in every:
                at = (a, slice(None), lanes(k))
                tn, ts, te, tw, tc, tu, tv = (
                    ref[at] + x + y for ref, x, y in zip(held, t3[k], t2[k])
                )
                tu = inv * (tu + rdu[at] * l1[0][k] * v1[(a, 0, *at[1:])])
                tv = inv * (tv + rdv[at] * l1[1][k] * v1[(a, 1, *at[1:])])
                wide, tall = 4.0 * tu + tv, tu + 4.0 * tv
                tn, ts, te, tw = tn - tall, ts - tall, te - wide, tw - wide
                facen[at] = tn
                faces[at] = ts
                accu[at] = tu + tv
                east_part.append(te)
                west_part.append(tw)
                rest.append(tn + ts + te + tw + (2.0 * coupling) * tc)
            moved = zip(rest, east(west_part), west(east_part))
            put(own, [0.5 * (r + x + y) for r, x, y in moved], a)

        rows(1, ROWS - 1, third)
        rows(2, ROWS - 2, second)
        rows(3, ROWS - 3, finish)

        for copy in back:
            copy.wait_recv()

        def edge_adjoint(a):
            m = get(m01, a)
            for comp, rd in ((0, rdu), (1, rdv)):
                p = [r * x for r, x in zip(get(rd, a), get(l4, a, comp))]
                put(p4, p, a, comp)
                put(q4, [x * y for x, y in zip(m, p)], a, comp)

        rows(-3, 0, edge_adjoint)
        rows(ROWS, ROWS + 3, edge_adjoint)
        for a in (0, HELD - 1):
            for comp in (0, 1):
                put(q4, [x * y for x, y in zip(get(m01, a), get(p4, a, comp))], a, comp)
        rows(-3, 1, third)
        rows(ROWS - 1, ROWS + 3, third)
        rows(-2, 2, second)
        rows(ROWS - 2, ROWS + 2, second)
        rows(-1, 3, finish)
        rows(ROWS - 3, ROWS + 1, finish)
        for k in every:
            at = (OFF - 1, slice(None), lanes(k))
            faces[at] = faces[at] + has_up * g4in[0, :, lanes(k)]
            at = (OFF + ROWS, slice(None), lanes(k))
            facen[at] = facen[at] + has_down * g4in[1, :, lanes(k)]

        def gradients(a):
            i = a - OFF
            for k in every:
                at = (slice(None), lanes(k))
                grad[(i, *at)] = -fric[(a, *at)] * accu[(a, *at)]
                both = own[(a, *at)] + 0.5 * (faces[(a - 1, *at)] + facen[(a + 1, *at)])
                grad[(i + ROWS, *at)] = stiff[(a, *at)] * both

        rows(0, ROWS, gradients)

        order = list(reversed(range(len(peers))))
        scatter = [
            send(grad.at[peers[k]], rsbuf.at[k], rsend.at[k], rrecv.at[k], {"epoch": peers[k]})
            for k in order
        ]
        mine = get(grad, ep)
        for copy, k in zip(scatter, order):
            copy.wait_recv()
            mine = [x + y for x, y in zip(mine, get(rsbuf, k))]
        put(total, mine, ep)
        put(summed, mine)
        sq = mine[0] * mine[0]
        for k in range(1, pieces):
            sq = sq + mine[k] * mine[k]
        sq = jnp.sum(sq, axis=0, keepdims=True)
        sqout[...] = sq
        sqin[ep] = sq

        squares = [
            send(sqout, sqin.at[ep], ssend.at[k], srecv.at[k], {"epoch": peers[k]}) for k in order
        ]
        gather = [
            send(summed, total.at[ep], gsend.at[k], grecv.at[k], {"epoch": peers[k]}) for k in order
        ]
        for copy in squares:
            copy.wait_recv()
        tot_q, tot_r = sqin[0], sqin[n_epoch // 2]
        for k in range(1, n_epoch // 2):
            tot_q = tot_q + sqin[k]
            tot_r = tot_r + sqin[n_epoch // 2 + k]
        rowout[0] = tot_q
        rowout[1] = tot_r
        across = [
            send(rowout, rowin.at[k - 1], tsend.at[k - 1], trecv.at[k - 1], {"row": lax.rem(me + k, n_row)})
            for k in range(1, n_row)
        ]
        for k, copy in enumerate(across):
            copy.wait_recv()
            tot_q = tot_q + rowin[k, 0]
            tot_r = tot_r + rowin[k, 1]
        factors = []
        for tot in (tot_q, tot_r):
            mean = jnp.sum(tot, axis=1, keepdims=True) / cells
            factor = step_size / jnp.sqrt(mean + 1e-6)
            factors.append(jnp.broadcast_to(factor, (SUB, LANE)))
        for copy in gather:
            copy.wait_recv()

        def update(a):
            i = a - OFF
            for ref, old, shift, factor in (
                (outq, lfraw, 0, factors[0]), (outr, lrraw, ROWS, factors[1])
            ):
                g = get(total, i + shift)
                for k in every:
                    at = (pl.ds(k * SUB + i, SUB, stride=span), slice(None))
                    ref[at] = old[at] - factor * g[k]

        rows(0, ROWS, update)

        for copy in halo + back + scatter + squares + gather + across:
            copy.wait_send()

    return kernel


def tiles(x):
    lead = x.shape[:-2]
    x = x.reshape(*lead, ROWS, x.shape[-1] // LANE, LANE)
    return jnp.swapaxes(x, -2, -3).reshape(-1, LANE)


def solution(mesh):
    n_epoch, n_row = mesh.shape["epoch"], mesh.shape["row"]

    def on_device(forcing, observed, log_friction, log_rheology, grounded):
        cols = forcing.shape[-1]
        width = cols // SUB
        raw_rows = ROWS * cols // LANE
        row = pltpu.VMEM((HELD, SUB, width), jnp.float32)
        pair = pltpu.VMEM((HELD, 2, SUB, width), jnp.float32)
        plain = lambda *lead: pltpu.VMEM((*lead, SUB, width), jnp.float32)
        dma = lambda n: pltpu.SemaphoreType.DMA((n,))
        scratch = [
            pltpu.VMEM((2 * raw_rows, LANE), jnp.float32),
            pltpu.VMEM((2 * raw_rows, LANE), jnp.float32),
            pltpu.VMEM((raw_rows, LANE), jnp.float32),
            pltpu.VMEM((raw_rows, LANE), jnp.float32),
            pltpu.VMEM((raw_rows, LANE), jnp.int32),
            row, row, pair, row, row, row, row, row, row, row,
            pair, pair, pair, pair,
            *([pair] * 9),
            *([row] * 7),
            row, row, row, plain(n_epoch), plain(2), plain(2),
            plain(n_epoch - 1), plain(), plain(n_epoch),
            pltpu.VMEM((1, LANE), jnp.float32),
            pltpu.VMEM((n_epoch, 1, LANE), jnp.float32),
            pltpu.VMEM((2, 1, LANE), jnp.float32),
            pltpu.VMEM((n_row - 1, 2, 1, LANE), jnp.float32),
            dma(5), dma(6), dma(6), dma(6), dma(6),
            *([dma(n_epoch - 1)] * 6),
            *([dma(n_row - 1)] * 2),
        ]
        shape = jax.ShapeDtypeStruct((raw_rows, LANE), jnp.float32)
        outs = pl.pallas_call(
            make_kernel(n_epoch, n_row, cols),
            out_shape=(shape, shape),
            in_specs=[pl.BlockSpec(memory_space=pl.ANY)] * 5,
            out_specs=(pl.BlockSpec(memory_space=pltpu.VMEM),) * 2,
            scratch_shapes=scratch,
            compiler_params=pltpu.CompilerParams(
                collective_id=0, has_side_effects=True, vmem_limit_bytes=60 * 2**20
            ),
            name="inversion_step",
        )(*(tiles(x) for x in (forcing, observed, log_friction, log_rheology, grounded)))

        def whole(x):
            return jnp.swapaxes(x.reshape(cols // LANE, ROWS, LANE), 0, 1).reshape(ROWS, cols)

        return whole(outs[0]), whole(outs[1])

    in_specs = (
        P("epoch", None, "row", None),
        P("epoch", None, "row", None),
        P("row", None),
        P("row", None),
        P("row", None),
    )
    out_specs = (P("row", None), P("row", None))
    return jax.shard_map(
        on_device, mesh=mesh, in_specs=in_specs, out_specs=out_specs, check_vma=False
    )
```

time: 231 us -> 52.5 us (0.23)
  waiting for transfers between devices: 124 us -> 0 us
  Pallas kernels: 0 us -> 49.4 us
  starting transfers between devices: 46.8 us -> 0 us
  blocking collectives: 25.3 us -> 0 us
  between operations: 14.9 us -> 0.65 us
  other arithmetic: 12.6 us -> 0 us
  local copies, waits for them, and re-layouts: 6.81 us -> 2.34 us
    psum x1 -> x0, waiting for transfers between devices: 95.9 us -> none  [on_device(): summed = lax.psum(gradient, 'epoch')]
    pallas_call x0 -> x1, Pallas kernels: none -> 49.4 us  [on_device(): pl.pallas_call(make_kernel(n_epoch, n_row, cols), out_shape=(shape, shape...]
    ppermute x18 -> x0, starting transfers between devices: 46.8 us -> none  [the longest x9 24.3 us: padded(): before = lax.ppermute(last, axis, up)]
    ppermute x18 -> x0, waiting for transfers between devices: 28.2 us -> none  [the longest x9 26.1 us: padded(): after = lax.ppermute(first, axis, down)]
    psum x1 -> x0, blocking collectives: 25.3 us -> none  [on_device(): squares = lax.psum(jnp.sum(summed * summed, axis=(1, 2)), 'row')]
    mul x23 -> x0, other arithmetic: 2.8 us -> none  [the longest x4 0.73 us: jacobi_sweep(): face_west = 0.5 * (centre + shift_west(centre))]
    slice x25 -> x0, local copies, waits for them, and re-layouts: 2.59 us -> none  [the longest x22 2.48 us: shift_east(): return jnp.pad(field[..., 1:], widths)]
  transfers between devices with their start and end apart: 19 -> 0, of which waited for: 9 -> 0; matrix products, arithmetic and copies ran while one was open for 1% -> 0% of each run, Pallas kernels for 0% -> 0%
where the time goes in v1:
time: 52.5 us; the launch traced here: 52.3 us
  Pallas kernels  49.4 us (94%)
  local copies, waits for them, and re-layouts  2.34 us (4%)
  between operations  0.65 us (1%)
    pallas_call x1, Pallas kernels, on_device(): pl.pallas_call(make_kernel(n_epoch, n_row, cols), out_shape=(shape, shape...  49.4 us
    unnamed x4, local copies, waits for them, and re-layouts  2.34 us

profile of v1, /device:TPU:1, one launch (start us, length us, event | category | flops | bytes accessed | tf_op | source)
XLA Modules:
  0.0 52.3 jit_solution(16238497585103338525)
XLA Ops:
  0.6 49.4 %inversion_step.1 = (f32[384,128]{1,0:T(8,128)}, f32[384,128]{1,0:T(8,128)}) custom-call(f32[768,128]{1,0:T(8,128)} %bitcast.35, f32[768,128]{1,0:T(8,128)} %bitcast.36, f32[384,128]{1,0:T(8,128)} %bitcast.39, f32[384,128]{1,0:T(8,128)} %bitcast.40, s32[384,128]{1,0:T(8,128)} %bitcast.41), custom_call_target="tpu_custom_call" | custom-call | tf_op jit(solution)/shard_map/inversion_step/pallas_call | solution.py:475
  50.0 0.0 copy-start
  50.0 1.7 %copy.9 = f32[8,6144]{1,0:T(8,128)} copy(f32[8,6144]{1,0:T(8,128)} %bitcast.38) | data formatting | bytes 393216
  51.7 0.0 copy-done
  51.7 0.7 %copy.10 = f32[8,6144]{1,0:T(8,128)} copy(f32[8,6144]{1,0:T(8,128)S(1)} %bitcast.37) | data formatting | bytes 393216
Async XLA Ops:
  50.0 1.7 %copy-start = (f32[384,128]{1,0:T(8,128)S(1)}, f32[384,128]{1,0:T(8,128)}, u32[]{:S(2)}) copy-start(f32[384,128]{1,0:T(8,128)} %get-tuple-element.5) | copy-start | bytes 589828

commit v2 on v1

--- a/solution.py
+++ b/solution.py
@@ -23,6 +23,8 @@
     pieces = cols // (SUB * LANE)
     span = pieces * SUB
     side = math.isqrt(n_epoch)
+    split = n_epoch // ROWS
+    width = pieces // split
     cells = n_row * ROWS * cols
 
     def kernel(
@@ -33,7 +35,7 @@
         l4, p4, q4, l3, p3, q3, l2, p2, q2,
         accn, accs, acce, accw, accc, accu, accv,
         facen, faces, own, grad, g4out, g4in,
-        rsbuf, summed, total, sqout, sqin, rowout, rowin,
+        rsbuf, mid, lastbuf, total, sqout, sqin, rowout, rowin,
         load_sem, hsend, hrecv, asend, arecv, rsend, rrecv, gsend, grecv, ssend, srecv, tsend, trecv,
     ):
         me = lax.axis_index("row")
@@ -346,58 +348,113 @@
         for a in (0, HELD - 1):
             for comp in (0, 1):
                 put(q4, [x * y for x, y in zip(get(m01, a), get(p4, a, comp))], a, comp)
+        def gradients(a):
+            for k in every:
+                at = (slice(None), lanes(k))
+                to = (split * (a - OFF) + k // width, slice(None), lanes(k % width))
+                grad[(0, *to)] = -fric[(a, *at)] * accu[(a, *at)]
+                both = own[(a, *at)] + 0.5 * (faces[(a - 1, *at)] + facen[(a + 1, *at)])
+                grad[(1, *to)] = stiff[(a, *at)] * both
+
+        here = (ex, ey)
+
+        def along(axis, k):
+            j = lax.rem(here[axis] + k, side)
+            return j, {"epoch": j * side + ey if axis == 0 else ex * side + j}
+
+        def first(f, k):
+            j, where = along(f, k)
+            n = f * (side - 1) + k - 1
+            return j, pltpu.make_async_remote_copy(
+                src_ref=grad.at[f, pl.ds(j * side, side)], dst_ref=rsbuf.at[f, k - 1],
+                send_sem=rsend.at[n], recv_sem=rrecv.at[n], device_id=where, device_id_type=MESH,
+            )
+
+        others = range(1, side)
+
+        def first_sends(low):
+            for k in others:
+                for f in (0, 1):
+                    j, copy = first(f, k)
+                    pl.when((j < side // 2) if low else (j >= side // 2))(copy.start)
+
         rows(-3, 1, third)
-        rows(ROWS - 1, ROWS + 3, third)
         rows(-2, 2, second)
-        rows(ROWS - 2, ROWS + 2, second)
         rows(-1, 3, finish)
-        rows(ROWS - 3, ROWS + 1, finish)
         for k in every:
             at = (OFF - 1, slice(None), lanes(k))
             faces[at] = faces[at] + has_up * g4in[0, :, lanes(k)]
+        rows(0, ROWS // 2, gradients)
+        first_sends(True)
+
+        rows(ROWS - 1, ROWS + 3, third)
+        rows(ROWS - 2, ROWS + 2, second)
+        rows(ROWS - 3, ROWS + 1, finish)
+        for k in every:
             at = (OFF + ROWS, slice(None), lanes(k))
             facen[at] = facen[at] + has_down * g4in[1, :, lanes(k)]
-
-        def gradients(a):
-            i = a - OFF
-            for k in every:
-                at = (slice(None), lanes(k))
-                grad[(i, *at)] = -fric[(a, *at)] * accu[(a, *at)]
-                both = own[(a, *at)] + 0.5 * (faces[(a - 1, *at)] + facen[(a + 1, *at)])
-                grad[(i + ROWS, *at)] = stiff[(a, *at)] * both
-
-        rows(0, ROWS, gradients)
+        rows(ROWS // 2, ROWS, gradients)
+        first_sends(False)
+
+        scatter = [first(f, k)[1] for k in others for f in (0, 1)]
+        for copy in scatter:
+            copy.wait_recv()
+        cut = [slice(k * LANE, (k + 1) * LANE) for k in range(width)]
+        for f in (0, 1):
+            for j in range(side):
+                for c in cut:
+                    x = grad[f, here[f] * side + j, :, c]
+                    for k in others:
+                        x = x + rsbuf[f, k - 1, j, :, c]
+                    mid[f, j, :, c] = x
+        for k in others:
+            for f in (0, 1):
+                j, where = along(1 - f, k)
+                n = (2 + f) * (side - 1) + k - 1
+                scatter.append(send(mid.at[f, j], lastbuf.at[f, k - 1], rsend.at[n], rrecv.at[n], where))
+        for copy in scatter[2 * (side - 1):]:
+            copy.wait_recv()
+        for f in (0, 1):
+            sq = jnp.zeros((SUB, LANE), jnp.float32)
+            for c in cut:
+                x = mid[f, here[1 - f], :, c]
+                for k in others:
+                    x = x + lastbuf[f, k - 1, :, c]
+                total[f, here[f] * side + here[1 - f], :, c] = x
+                sq = sq + x * x
+            sq = jnp.sum(sq, axis=0, keepdims=True)
+            sqout[f] = sq
+            sqin[ep, f] = sq
 
         order = list(reversed(range(len(peers))))
-        scatter = [
-            send(grad.at[peers[k]], rsbuf.at[k], rsend.at[k], rrecv.at[k], {"epoch": peers[k]})
-            for k in order
-        ]
-        mine = get(grad, ep)
-        for copy, k in zip(scatter, order):
-            copy.wait_recv()
-            mine = [x + y for x, y in zip(mine, get(rsbuf, k))]
-        put(total, mine, ep)
-        put(summed, mine)
-        sq = mine[0] * mine[0]
-        for k in range(1, pieces):
-            sq = sq + mine[k] * mine[k]
-        sq = jnp.sum(sq, axis=0, keepdims=True)
-        sqout[...] = sq
-        sqin[ep] = sq
-
         squares = [
             send(sqout, sqin.at[ep], ssend.at[k], srecv.at[k], {"epoch": peers[k]}) for k in order
         ]
-        gather = [
-            send(summed, total.at[ep], gsend.at[k], grecv.at[k], {"epoch": peers[k]}) for k in order
-        ]
+
+        gather, onward = [], []
+
+        def share(f, axis, source, slot, copies):
+            part = total.at[f, here[f] * side + source]
+            for k in others:
+                n = (slot * 2 + f) * (side - 1) + k - 1
+                copies.append(send(part, part, gsend.at[n], grecv.at[n], along(axis, k)[1]))
+
+        for f in (0, 1):
+            share(f, 1 - f, here[1 - f], 0, gather)
+        for f in (0, 1):
+            share(f, f, here[1 - f], 1, onward)
+        for k in others:
+            for f in (0, 1):
+                gather[f * (side - 1) + k - 1].wait_recv()
+                share(f, f, lax.rem(here[1 - f] + side - k, side), 1 + k, onward)
+        gather = gather + onward
+
         for copy in squares:
             copy.wait_recv()
-        tot_q, tot_r = sqin[0], sqin[n_epoch // 2]
-        for k in range(1, n_epoch // 2):
-            tot_q = tot_q + sqin[k]
-            tot_r = tot_r + sqin[n_epoch // 2 + k]
+        tot_q, tot_r = sqin[0, 0], sqin[0, 1]
+        for k in range(1, n_epoch):
+            tot_q = tot_q + sqin[k, 0]
+            tot_r = tot_r + sqin[k, 1]
         rowout[0] = tot_q
         rowout[1] = tot_r
         across = [
@@ -413,18 +470,16 @@
             mean = jnp.sum(tot, axis=1, keepdims=True) / cells
             factor = step_size / jnp.sqrt(mean + 1e-6)
             factors.append(jnp.broadcast_to(factor, (SUB, LANE)))
-        for copy in gather:
+        for copy in onward:
             copy.wait_recv()
 
         def update(a):
             i = a - OFF
-            for ref, old, shift, factor in (
-                (outq, lfraw, 0, factors[0]), (outr, lrraw, ROWS, factors[1])
-            ):
-                g = get(total, i + shift)
+            for f, (ref, old) in enumerate(((outq, lfraw), (outr, lrraw))):
                 for k in every:
                     at = (pl.ds(k * SUB + i, SUB, stride=span), slice(None))
-                    ref[at] = old[at] - factor * g[k]
+                    g = total[f, split * i + k // width, :, lanes(k % width)]
+                    ref[at] = old[at] - factors[f] * g
 
         rows(0, ROWS, update)
 
@@ -450,6 +505,8 @@
         row = pltpu.VMEM((HELD, SUB, width), jnp.float32)
         pair = pltpu.VMEM((HELD, 2, SUB, width), jnp.float32)
         plain = lambda *lead: pltpu.VMEM((*lead, SUB, width), jnp.float32)
+        side = math.isqrt(n_epoch)
+        part = lambda *lead: pltpu.VMEM((*lead, SUB, width * ROWS // n_epoch), jnp.float32)
         dma = lambda n: pltpu.SemaphoreType.DMA((n,))
         scratch = [
             pltpu.VMEM((2 * raw_rows, LANE), jnp.float32),
@@ -461,14 +518,16 @@
             pair, pair, pair, pair,
             *([pair] * 9),
             *([row] * 7),
-            row, row, row, plain(n_epoch), plain(2), plain(2),
-            plain(n_epoch - 1), plain(), plain(n_epoch),
-            pltpu.VMEM((1, LANE), jnp.float32),
-            pltpu.VMEM((n_epoch, 1, LANE), jnp.float32),
+            row, row, row, part(2, n_epoch), plain(2), plain(2),
+            part(2, side - 1, side), part(2, side), part(2, side - 1), part(2, n_epoch),
+            pltpu.VMEM((2, 1, LANE), jnp.float32),
+            pltpu.VMEM((n_epoch, 2, 1, LANE), jnp.float32),
             pltpu.VMEM((2, 1, LANE), jnp.float32),
             pltpu.VMEM((n_row - 1, 2, 1, LANE), jnp.float32),
             dma(5), dma(6), dma(6), dma(6), dma(6),
-            *([dma(n_epoch - 1)] * 6),
+            *([dma(4 * (side - 1))] * 2),
+            *([dma(2 * (side + 1) * (side - 1))] * 2),
+            *([dma(n_epoch - 1)] * 2),
             *([dma(n_row - 1)] * 2),
         ]
         shape = jax.ShapeDtypeStruct((raw_rows, LANE), jnp.float32)

time: 52.5 us -> 54.1 us (1.030)
  Pallas kernels: 49.4 us -> 51 us
    pallas_call x1, Pallas kernels: 49.4 us -> 51 us  [on_device(): pl.pallas_call(make_kernel(n_epoch, n_row, cols), out_shape=(shape, shape...]
where the time goes in v2:
time: 54.1 us; the launch traced here: 54 us
  Pallas kernels  51 us (94%)
  local copies, waits for them, and re-layouts  2.34 us (4%)
  between operations  0.65 us (1%)
    pallas_call x1, Pallas kernels, on_device(): pl.pallas_call(make_kernel(n_epoch, n_row, cols), out_shape=(shape, shape...  51 us
    unnamed x4, local copies, waits for them, and re-layouts  2.34 us

profile of v2, /device:TPU:1, one launch (start us, length us, event | category | flops | bytes accessed | tf_op | source)
XLA Modules:
  0.0 54.0 jit_solution(14356296330198908978)
XLA Ops:
  0.6 51.0 %inversion_step.1 = (f32[384,128]{1,0:T(8,128)}, f32[384,128]{1,0:T(8,128)}) custom-call(f32[768,128]{1,0:T(8,128)} %bitcast.35, f32[768,128]{1,0:T(8,128)} %bitcast.36, f32[384,128]{1,0:T(8,128)} %bitcast.39, f32[384,128]{1,0:T(8,128)} %bitcast.40, s32[384,128]{1,0:T(8,128)} %bitcast.41), custom_call_target="tpu_custom_call" | custom-call | tf_op jit(solution)/shard_map/inversion_step/pallas_call | solution.py:534
  51.6 0.0 copy-start
  51.6 1.7 %copy.9 = f32[8,6144]{1,0:T(8,128)} copy(f32[8,6144]{1,0:T(8,128)} %bitcast.38) | data formatting | bytes 393216
  53.3 0.0 copy-done
  53.3 0.7 %copy.10 = f32[8,6144]{1,0:T(8,128)} copy(f32[8,6144]{1,0:T(8,128)S(1)} %bitcast.37) | data formatting | bytes 393216
Async XLA Ops:
  51.6 1.7 %copy-start = (f32[384,128]{1,0:T(8,128)S(1)}, f32[384,128]{1,0:T(8,128)}, u32[]{:S(2)}) copy-start(f32[384,128]{1,0:T(8,128)} %get-tuple-element.5) | copy-start | bytes 589828

commit v3 on v1

--- a/solution.py
+++ b/solution.py
@@ -102,11 +102,14 @@
             return [a - b for a, b in zip(east(d), west(d))]
 
         def rows(lo, hi, body):
-            def step(a, carry):
-                body(a)
+            by = 2 if (hi - lo) % 2 == 0 else 1
+
+            def step(n, carry):
+                for m in range(by):
+                    body(lo + OFF + n * by + m)
                 return carry
 
-            lax.fori_loop(lo + OFF, hi + OFF, step, 0)
+            lax.fori_loop(0, (hi - lo) // by, step, 0)
 
         loads[0].wait()
 

time: 52.5 us -> 50.2 us (0.956)
  Pallas kernels: 49.4 us -> 47.1 us
    pallas_call x1, Pallas kernels: 49.4 us -> 47.1 us  [on_device(): pl.pallas_call(make_kernel(n_epoch, n_row, cols), out_shape=(shape, shape...]
where the time goes in v3:
time: 50.2 us; the launch traced here: 50.1 us
  Pallas kernels  47.1 us (94%)
  local copies, waits for them, and re-layouts  2.34 us (5%)
  between operations  0.65 us (1%)
    pallas_call x1, Pallas kernels, on_device(): pl.pallas_call(make_kernel(n_epoch, n_row, cols), out_shape=(shape, shape...  47.1 us
    unnamed x4, local copies, waits for them, and re-layouts  2.34 us

profile of v3, /device:TPU:1, one launch (start us, length us, event | category | flops | bytes accessed | tf_op | source)
XLA Modules:
  0.0 50.1 jit_solution(6567387027544892873)
XLA Ops:
  0.6 47.1 %inversion_step.1 = (f32[384,128]{1,0:T(8,128)}, f32[384,128]{1,0:T(8,128)}) custom-call(f32[768,128]{1,0:T(8,128)} %bitcast.35, f32[768,128]{1,0:T(8,128)} %bitcast.36, f32[384,128]{1,0:T(8,128)} %bitcast.39, f32[384,128]{1,0:T(8,128)} %bitcast.40, s32[384,128]{1,0:T(8,128)} %bitcast.41), custom_call_target="tpu_custom_call" | custom-call | tf_op jit(solution)/shard_map/inversion_step/pallas_call | solution.py:478
  47.8 0.0 copy-start
  47.8 1.7 %copy.9 = f32[8,6144]{1,0:T(8,128)} copy(f32[8,6144]{1,0:T(8,128)} %bitcast.38) | data formatting | bytes 393216
  49.4 0.0 copy-done
  49.4 0.7 %copy.10 = f32[8,6144]{1,0:T(8,128)} copy(f32[8,6144]{1,0:T(8,128)S(1)} %bitcast.37) | data formatting | bytes 393216
Async XLA Ops:
  47.8 1.7 %copy-start = (f32[384,128]{1,0:T(8,128)S(1)}, f32[384,128]{1,0:T(8,128)}, u32[]{:S(2)}) copy-start(f32[384,128]{1,0:T(8,128)} %get-tuple-element.5) | copy-start | bytes 589828

commit v4 on v3

--- a/solution.py
+++ b/solution.py
@@ -101,8 +101,8 @@
             d = [s - n for s, n in zip(south, north)]
             return [a - b for a, b in zip(east(d), west(d))]
 
-        def rows(lo, hi, body):
-            by = 2 if (hi - lo) % 2 == 0 else 1
+        def rows(lo, hi, body, by=2):
+            by = by if (hi - lo) % by == 0 else 1
 
             def step(n, carry):
                 for m in range(by):
@@ -116,7 +116,7 @@
         def own_stiff(a):
             put(stiff, [jnp.exp(x) for x in raw(lrraw, a - OFF)], a)
 
-        rows(0, ROWS, own_stiff)
+        rows(0, ROWS, own_stiff, 4)
         loads[1].wait()
         loads[2].wait()
 
@@ -124,14 +124,14 @@
             held_up = zip(raw(grraw, a - OFF), raw(lfraw, a - OFF))
             put(fric, [g.astype(jnp.float32) * jnp.exp(x) for g, x in held_up], a)
 
-        rows(0, ROWS, own_fric)
+        rows(0, ROWS, own_fric, 4)
         loads[3].wait()
 
         def own_force(a):
             put(force, raw(fraw, a - OFF, 0), a, 0)
             put(force, raw(fraw, a - OFF, 1), a, 1)
 
-        rows(0, ROWS, own_force)
+        rows(0, ROWS, own_force, 4)
 
         pl.semaphore_wait(barrier, n_row - 1 + len(peers))
 
@@ -228,7 +228,7 @@
                 put(p4, p, a, comp)
                 put(q4, [x * y for x, y in zip(m, p)], a, comp)
 
-        rows(0, ROWS, last_adjoint)
+        rows(0, ROWS, last_adjoint, 4)
         back = [
             send(l4.at[pl.ds(OFF, 3)], l4.at[pl.ds(OFF + ROWS, 3)], asend.at[0], arecv.at[0], {"row": up}),
             send(l4.at[pl.ds(OFF + ROWS - 3, 3)], l4.at[pl.ds(OFF - 3, 3)], asend.at[1], arecv.at[1], {"row": down}),
@@ -369,7 +369,7 @@
                 both = own[(a, *at)] + 0.5 * (faces[(a - 1, *at)] + facen[(a + 1, *at)])
                 grad[(i + ROWS, *at)] = stiff[(a, *at)] * both
 
-        rows(0, ROWS, gradients)
+        rows(0, ROWS, gradients, 4)
 
         order = list(reversed(range(len(peers))))
         scatter = [
@@ -429,7 +429,7 @@
                     at = (pl.ds(k * SUB + i, SUB, stride=span), slice(None))
                     ref[at] = old[at] - factor * g[k]
 
-        rows(0, ROWS, update)
+        rows(0, ROWS, update, 4)
 
         for copy in halo + back + scatter + squares + gather + across:
             copy.wait_send()

time: 50.2 us -> 50.2 us (level)
  no operation moved by 1% of the time
where the time goes in v4:
time: 50.2 us; the launch traced here: 50.1 us
  Pallas kernels  47.1 us (94%)
  local copies, waits for them, and re-layouts  2.34 us (5%)
  between operations  0.65 us (1%)
    pallas_call x1, Pallas kernels, on_device(): pl.pallas_call(make_kernel(n_epoch, n_row, cols), out_shape=(shape, shape...  47.1 us
    unnamed x4, local copies, waits for them, and re-layouts  2.34 us

profile of v4, /device:TPU:1, one launch (start us, length us, event | category | flops | bytes accessed | tf_op | source)
XLA Modules:
  0.0 50.1 jit_solution(4453873206905246334)
XLA Ops:
  0.6 47.1 %inversion_step.1 = (f32[384,128]{1,0:T(8,128)}, f32[384,128]{1,0:T(8,128)}) custom-call(f32[768,128]{1,0:T(8,128)} %bitcast.35, f32[768,128]{1,0:T(8,128)} %bitcast.36, f32[384,128]{1,0:T(8,128)} %bitcast.39, f32[384,128]{1,0:T(8,128)} %bitcast.40, s32[384,128]{1,0:T(8,128)} %bitcast.41), custom_call_target="tpu_custom_call" | custom-call | tf_op jit(solution)/shard_map/inversion_step/pallas_call | solution.py:478
  47.7 0.0 copy-start
  47.7 1.7 %copy.9 = f32[8,6144]{1,0:T(8,128)} copy(f32[8,6144]{1,0:T(8,128)} %bitcast.38) | data formatting | bytes 393216
  49.4 0.0 copy-done
  49.4 0.7 %copy.10 = f32[8,6144]{1,0:T(8,128)} copy(f32[8,6144]{1,0:T(8,128)S(1)} %bitcast.37) | data formatting | bytes 393216
Async XLA Ops:
  47.7 1.7 %copy-start = (f32[384,128]{1,0:T(8,128)S(1)}, f32[384,128]{1,0:T(8,128)}, u32[]{:S(2)}) copy-start(f32[384,128]{1,0:T(8,128)} %get-tuple-element.5) | copy-start | bytes 589828
